TPU v7x, 256 devices: a whole 4x4x8 slice. The times are simulated.
256 devices in a mesh: ctx: 16 (over x, y), head: 16 (over z, core).
Axes of the slice: x: 4, y: 4, z: 8, core: 2. Of those that a mesh axis runs over, the one named last changes fastest.
Arguments:
- tokens: bfloat16 [8192, 8192], P('ctx'), may hold values from -6 to 6
- w_zx: bfloat16 [8192, 2, 8192], P('ctx', None, 'head'), may hold values from -0.0625 to 0.0625
- zx_scale: float32 [2, 8192], P(None, 'head'), may hold values from 0.5 to 2
- w_bc: bfloat16 [8192, 8, 512], P('ctx'), may hold values from -0.0625 to 0.0625
- bc_scale: float32 [8, 512], replicated, may hold values from 0.5 to 2
- w_dt: bfloat16 [8192, 128], P('ctx', 'head'), may hold values from -0.0625 to 0.0625
- conv_x: float32 [5, 8192], P(None, 'head'), may hold values from -3 to 3
- conv_bc: float32 [5, 8, 512], replicated, may hold values from -3 to 3
- tail_x: bfloat16 [3, 8192], P(None, 'head'), may hold values from -6 to 6
- tail_bc: bfloat16 [3, 8, 512], replicated, may hold values from -6 to 6
- head_params: float32 [3, 128], P(None, 'head'), may hold values from -12 to 2, as said below
- init_state: float32 [128, 64, 256], P('head'), may hold values from -1.5 to 1.5
- norm_gain: float32 [8192], P('head'), may hold values from 0.5 to 1.5
Outputs:
- mixed: bfloat16 [8192, 8192], P('ctx', 'head')
Inputs may be any that keep to these rules, and one draw needn't show every extreme that they name: `head_params`: row 0 lies in -3.5 to -2.5 and row 2 in 0.5 to 1.5.
All inputs are finite; a program needn't handle non-finite values.
Results may differ from a plain program's by a relative error of at most 0.0052.
Values may be sent and summed in bfloat16 or wider, within the bound.
A program may use at most 256 MiB of HBM per device.

v0:
```python
import jax
import jax.numpy as jnp
from jax import lax
from jax.sharding import PartitionSpec as P

H = 128
P_SIZE = 64
N = 256
G = 8
K = 4


def passed_along(x, axis, by):
    length = lax.axis_size(axis)
    pairs = [(i, i + by) for i in range(length) if 0 <= i + by < length]
    return lax.ppermute(x, axis, pairs)


def prefix(part, axis, combine, identity):
    place = lax.axis_index(axis)
    gathered = jax.tree.map(lambda a: lax.all_gather(a, axis), part)
    state = jax.tree.map(lambda a, e: jnp.zeros_like(a) + jnp.asarray(e, a.dtype), part, identity)

    def one(lap, state):
        return combine(
            state, jax.tree.map(lambda a: lax.dynamic_index_in_dim(a, lap, 0, False), gathered)
        )

    return lax.fori_loop(0, place, one, state)


def conv_silu(values, before, taps):
    length = values.shape[0]
    padded = jnp.concatenate([before, values], 0).astype(jnp.float32)
    summed = taps[K]
    for tap_index in range(K):
        summed = summed + taps[tap_index] * padded[tap_index : tap_index + length]
    return jax.nn.silu(summed).astype(jnp.bfloat16)


def pick_group(values, group_index, axis_index):
    chosen = lax.dynamic_index_in_dim(values, group_index, axis_index, keepdims=False)
    return chosen


def body(
    tokens,
    w_zx,
    zx_scale,
    w_bc,
    bc_scale,
    w_dt,
    conv_x,
    conv_bc,
    tail_x,
    tail_bc,
    head_params,
    init_state,
    norm_gain,
):
    highest = lax.Precision.HIGHEST
    tok_rows = tokens.shape[0]
    local_heads = head_params.shape[1]
    channels = local_heads * P_SIZE
    per_group = H // G
    group_index = lax.axis_index("head") * local_heads // per_group
    bc_rows = pick_group(w_bc, group_index, 1)
    bc_scales = pick_group(bc_scale, group_index, 0)
    bc_taps = pick_group(conv_bc, group_index, 1)
    bc_tail = pick_group(tail_bc, group_index, 1)
    zx_rows = w_zx.reshape(w_zx.shape[0], 2 * channels)
    pieces = (
        lax.all_gather(zx_rows, "ctx", axis=0, tiled=True),
        lax.all_gather(bc_rows, "ctx", axis=0, tiled=True),
        lax.all_gather(w_dt, "ctx", axis=0, tiled=True),
    )
    zx_sum, bc_sum, step_sum = tuple(
        (jnp.dot(tokens, piece, preferred_element_type=jnp.float32) for piece in pieces)
    )
    zx_val = (zx_sum.reshape(tok_rows, 2, channels) * zx_scale).astype(jnp.bfloat16)
    gate = zx_val[:, 0]
    inner_in = zx_val[:, 1]
    bc_val = (bc_sum * bc_scales).astype(jnp.bfloat16)
    step_size = jax.nn.softplus(step_sum + head_params[0])
    edge = jnp.concatenate([inner_in[tok_rows - (K - 1) :], bc_val[tok_rows - (K - 1) :]], 1)
    arrived = passed_along(edge, "ctx", 1)
    previous = jnp.concatenate([tail_x, bc_tail], 1)
    arrived = jnp.where(lax.axis_index("ctx") == 0, previous, arrived)
    xconv = conv_silu(inner_in, arrived[:, :channels], conv_x)
    bconv = conv_silu(bc_val, arrived[:, channels:], bc_taps)
    b_part = bconv[:, :N]
    c_part = bconv[:, N:]
    x_heads = xconv.reshape(tok_rows, local_heads, P_SIZE).astype(jnp.float32)
    rate = -jnp.exp(head_params[1]) * step_size
    cumul = jnp.cumsum(rate, 0)
    cumul_t = cumul.T
    order = jnp.arange(tok_rows)
    lower = order[:, None] >= order[None, :]
    spread = cumul_t[:, :, None] - cumul_t[:, None, :]
    decay = jnp.where(lower[None], jnp.exp(jnp.minimum(spread, 0.0)), 0.0)
    scores = jnp.dot(c_part, b_part.T, preferred_element_type=jnp.float32)
    weights = decay * scores[None] * step_size.T[:, None, :]
    inner = jnp.einsum("hts,shp->thp", weights, x_heads, precision=highest)
    log_total = cumul[tok_rows - 1]
    fade = jnp.exp(log_total[None, :] - cumul) * step_size
    local_state = jnp.einsum(
        "sh,shp,sn->hpn", fade, x_heads, b_part.astype(jnp.float32), precision=highest
    )

    def combine(earlier, later):
        return (earlier[0] + later[0], jnp.exp(later[0])[:, None, None] * earlier[1] + later[1])

    before_log, before_state = prefix(
        (log_total, local_state),
        "ctx",
        combine,
        (jnp.zeros_like(log_total), jnp.zeros_like(local_state)),
    )
    incoming = jnp.exp(before_log)[:, None, None] * init_state + before_state
    carried = (
        jnp.einsum("tn,hpn->thp", c_part.astype(jnp.float32), incoming, precision=highest)
        * jnp.exp(cumul)[:, :, None]
    )
    y_val = inner + carried + head_params[2][None, :, None] * x_heads
    gated = y_val.reshape(tok_rows, channels) * jax.nn.silu(gate.astype(jnp.float32))
    squares = jnp.sum(gated * gated, axis=1)
    slot_hits = (jnp.arange(G) == group_index).astype(jnp.float32)
    placed = slot_hits[:, None] * squares[None, :]
    group_sums = lax.psum(placed, "head")
    totals = lax.dynamic_index_in_dim(group_sums, group_index, 0, keepdims=False)
    meansq = totals / (per_group * P_SIZE)
    mixed = gated * lax.rsqrt(meansq + 1e-05)[:, None] * norm_gain
    return mixed.astype(jnp.bfloat16)


def solution(mesh):
    return jax.shard_map(
        body,
        mesh=mesh,
        in_specs=(
            P("ctx", None),
            P("ctx", None, "head"),
            P(None, "head"),
            P("ctx", None, None),
            P(),
            P("ctx", "head"),
            P(None, "head"),
            P(),
            P(None, "head"),
            P(),
            P(None, "head"),
            P("head", None, None),
            P("head"),
        ),
        out_specs=P("ctx", "head"),
        check_vma=False,
    )
```

profile of v0, /device:TPU:30, one launch (start us, length us, event | category | flops | bytes accessed | tf_op | source)
XLA Modules:
  0.0 391.0 jit_solution(2558766528780283261)
XLA Ops:
  6.5 3.3 constant_dynamic-slice_fusion.8
  9.8 0.9 copy.38
  10.7 0.0 all-gather.9.cloned.1.call-update
  10.8 0.0 all-gather.7.cloned.1.call-start
  10.8 2.5 copy.40
  13.4 0.0 all-gather.7.cloned.1.call-update
  13.4 0.0 all-gather.11.cloned.1.call-start
  13.5 21.8 %all_gather.20 = bf16[8192,8]{0,1:T(8,128)(2,1)S(1)} all-gather(bf16[512,8]{0,1:T(8,128)(2,1)} %param.20), channel_id=1, replica_groups=mesh['ctx'=16,'head'=16] {'ctx'}, dimensions={0}, use_global_device_ids=true | all-gather | bytes 139264 | tf_op jit(solution)/shard_map/all_gather | solution.py:75
  35.3 0.8 slice_bitcast_fusion.2
  36.1 5.7 %convolution_add_fusion = f32[512,8]{0,1:T(8,128)S(1)} fusion(bf16[512,8192]{1,0:T(8,128)(2,1)} %param.15, bf16[8192,8]{0,1:T(8,128)(2,1)S(1)} %all_gather.20, f32[8]{0:T(128)S(1)} %get-tuple-element.93), kind=kOutput, calls=%fused_computation.30 | convolution fusion | flops 67112960 | bytes 8536096 | tf_op jit(solution)/shard_map/dot_general | solution.py:78
  41.8 0.1 multiply_bitcast_fusion
  41.9 1.1 reduce-window.6
  43.0 0.2 slice_reduce_fusion
  43.2 0.7 constant_dynamic-slice_fusion.7
  44.0 0.1 fusion.66
  44.0 0.2 slice_reduce_fusion.1
  44.2 0.8 constant_dynamic-slice_fusion.4
  45.0 0.1 fusion.57
  45.1 42.5 %all-gather.9.cloned.1.call-done = bf16[8192,1,512]{2,0,1:T(8,128)(2,1)} async-done(((bf16[512,1,512]{2,0,1:T(8,128)(2,1)}), bf16[8192,1,512]{2,0,1:T(8,128)(2,1)}) %all-gather.9.cloned.1.call-update) | async-done | bytes 8388624 | tf_op jit(solution)/shard_map/all_gather | solution.py:74
  87.6 10.2 %fusion.27 = bf16[512,512]{1,0:T(8,128)(2,1)S(1)} fusion(bf16[512,8192]{1,0:T(8,128)(2,1)} %param.15, bf16[8192,1,512]{2,0,1:T(8,128)(2,1)} %all-gather.9.cloned.1.call-done, f32[512]{0:T(512)S(1)} %bitcast.142), kind=kOutput, calls=%fused_computation.29 | convolution fusion | flops 4295491584 | bytes 17303552 | tf_op jit(solution)/shard_map/dot_general | solution.py:78
  97.9 0.0 copy-start.4
  97.9 0.8 copy-done.4
  98.7 107.3 %all-gather.7.cloned.1.call-done = bf16[8192,1024]{1,0:T(8,128)(2,1)} async-done(((bf16[512,1024]{1,0:T(8,128)(2,1)}), bf16[8192,1024]{1,0:T(8,128)(2,1)}) %all-gather.7.cloned.1.call-update) | async-done | bytes 16777232 | tf_op jit(solution)/shard_map/all_gather | solution.py:73
  206.0 14.3 %fusion.69 = f32[512,1024]{1,0:T(8,128)S(1)} fusion(bf16[512,8192]{1,0:T(8,128)(2,1)} %param.15, bf16[8192,1024]{1,0:T(8,128)(2,1)} %all-gather.7.cloned.1.call-done), kind=kOutput, calls=%fused_computation.115 | convolution fusion | flops 8589934592 | bytes 27262976 | tf_op jit(solution)/shard_map/dot_general | solution.py:78
  220.4 0.3 fusion.15
  220.7 1.5 collective-permute-start
  222.2 0.2 slice_convert_fusion
  222.4 3.9 collective-permute-done
  226.3 0.2 maximum_convert_fusion
  226.5 1.5 multiply_convert_fusion.1
  228.0 2.1 copy.31
  230.0 0.7 multiply_convert_fusion
  230.7 0.8 copy-done.1
  231.5 2.5 fusion.30
  234.0 0.0 all-gather.11.cloned.1.call-update
  234.0 21.3 %all-gather.2 = f32[16,1,8]{2,1,0:T(1,128)S(1)} all-gather(f32[1,1,8]{2,1,0:T(1,128)S(1)} %bitcast.141), channel_id=1, replica_groups=mesh['ctx'=16,'head'=16] {'ctx'}, dimensions={0}, use_global_device_ids=true | all-gather | bytes 544 | tf_op jit(solution)/shard_map/all_gather | solution.py:21
  255.3 0.1 iota_compare_fusion
  255.4 0.1 add_bitcast_fusion.1
  255.5 1.4 copy.35
  256.9 1.4 fusion.53
  258.2 8.7 %fusion.16 = f32[512,8,64]{0,2,1:T(8,128)} fusion(bf16[512,8,64]{0,2,1:T(8,128)(2,1)} %bitcast.122, f32[8,512]{1,0:T(8,128)S(1)} %get-tuple-element.83, f32[512,512]{1,0:T(8,128)S(1)} %fusion.53, f32[8,512]{1,0:T(8,128)S(1)} %add_bitcast_fusion.1, pred[512,512]{1,0:T(8,128)(4,1)S(1)} %iota_compare_fusion), kind=kOutput, calls=%fused_computation.21 | convolution fusion | flops 1621098496 | bytes 2916352 | tf_op jit(solution)/shard_map/hts,shp->thp/dot_general | solution.py:103
  266.9 44.0 %all-gather.11.cloned.1.call-done = f32[128,64,256]{2,1,0:T(8,128)} async-done(((f32[8,64,256]{2,1,0:T(8,128)}), f32[128,64,256]{2,1,0:T(8,128)}) %all-gather.11.cloned.1.call-update) | async-done | bytes 8388624 | tf_op jit(solution)/shard_map/all_gather | solution.py:21
  311.0 0.0 copy-start.9
  311.0 18.8 %while.12 = (s32[]{:T(128)}, f32[8]{0:T(128)S(1)}, f32[8,64,256]{2,1,0:T(8,128)S(1)}, s32[]{:T(128)}, f32[16,8]{1,0:T(8,128)S(1)}, /*index=5*/f32[16,8,64,256]{3,2,1,0:T(8,128)}, s32[]{:T(128)}, s32[]{:T(128)}, s32[]{:T(128)}) while((s32[]{:T(128)}, f32[8]{0:T(128)S(1)}, f32[8,64,256]{2,1,0:T(8,128)S(1)}, s32[]{:T(128)}, ...), condition=%wide.region_3.4_spmd, body=%wide.region_2.3_spmd.sunk | while | flops 262157 | bytes 1573167 | solution.py:29
  311.1 1.2 bitcast_add_fusion.3
  312.3 1.2 bitcast_add_fusion.3
  313.6 1.2 bitcast_add_fusion.3
  314.8 1.2 bitcast_add_fusion.3
  316.1 1.2 bitcast_add_fusion.3
  317.3 1.2 bitcast_add_fusion.3
  318.6 1.2 bitcast_add_fusion.3
  319.8 1.2 bitcast_add_fusion.3
  321.1 1.2 bitcast_add_fusion.3
  322.3 1.2 bitcast_add_fusion.3
  323.6 1.2 bitcast_add_fusion.3
  324.9 1.2 bitcast_add_fusion.3
  326.1 1.2 bitcast_add_fusion.3
  327.4 1.2 bitcast_add_fusion.3
  328.6 1.2 bitcast_add_fusion.3
  329.9 3.6 multiply_reduce_fusion
  333.5 1.6 copy.34
  335.1 0.1 broadcast_multiply_fusion
  335.1 48.1 %psum.7 = f32[8,512]{1,0:T(8,128)S(1)} all-reduce(f32[8,512]{1,0:T(8,128)S(1)} %broadcast_multiply_fusion), channel_id=1, replica_groups=mesh['ctx'=16,'head'=16] {'head'}, use_global_device_ids=true, to_apply=%region_5.6 | all-reduce | flops 4096 | bytes 32768 | tf_op jit(solution)/shard_map/psum | solution.py:129
  383.3 1.2 fusion.45
  (47 shorter events, 0.5 us)
Async XLA Ops:
  6.5 6.9 %copy-start = (bf16[3,8,512]{2,1,0:T(8,128)(2,1)S(1)}, bf16[3,8,512]{2,1,0:T(8,128)(2,1)}, u32[]{:S(2)}) copy-start(bf16[3,8,512]{2,1,0:T(8,128)(2,1)} %param.24) | copy-start | bytes 73732
  6.5 38.5 %copy-start.6 = (f32[5,512]{1,0:T(8,128)S(1)}, f32[5,512]{1,0:T(8,128)}, u32[]{:S(2)}) copy-start(f32[5,512]{1,0:T(8,128)} %param.21) | copy-start | bytes 30724
  6.5 81.1 %all-gather.9.cloned.1.call-start = ((), (), s32[]{:S(2)}) async-start(), calls=%async_computation.1 | async-start | bytes 8912896 | tf_op jit(solution)/shard_map/all_gather | solution.py:74
  10.8 195.3 %all-gather.7.cloned.1.call-start = ((), (), s32[]{:S(2)}) async-start(), calls=%async_computation | async-start | bytes 17825792 | tf_op jit(solution)/shard_map/all_gather | solution.py:73
  13.4 297.6 %all-gather.11.cloned.1.call-start = ((), (), s32[]{:S(2)}) async-start(), calls=%async_computation.2 | async-start | bytes 8912896 | tf_op jit(solution)/shard_map/all_gather | solution.py:21
  97.9 0.8 copy-start.4
  98.7 121.7 %copy-start.7 = (f32[2,512]{1,0:T(2,128)S(1)}, f32[2,512]{1,0:T(2,128)}, u32[]{:S(2)}) copy-start(f32[2,512]{1,0:T(2,128)} %param.17) | copy-start | bytes 12292
  98.7 127.6 %copy-start.8 = (bf16[3,512]{1,0:T(4,128)(2,1)S(1)}, bf16[3,512]{1,0:T(4,128)(2,1)}, u32[]{:S(2)}) copy-start(bf16[3,512]{1,0:T(4,128)(2,1)} %param.23) | copy-start | bytes 9220
  206.0 20.2 %copy-start.5 = (bf16[512,512]{1,0:T(8,128)(2,1)S(1)}, bf16[512,512]{1,0:T(8,128)(2,1)}, u32[]{:S(2)}) copy-start(bf16[512,512]{1,0:T(8,128)(2,1)} %copy-done.4) | copy-start | bytes 1572868
  220.7 5.5 %collective-permute-start = (bf16[3,1024]{1,0:T(4,128)(2,1)S(1)}, bf16[3,1024]{1,0:T(4,128)(2,1)S(1)}, u32[]{:S(2)}, u32[]{:S(2)}) collective-permute-start(bf16[3,1024]{1,0:T(4,128)(2,1)S(1)} %pad_maximum_fusion), channel_id=1, source_target_pairs={{0,16},{16,32},{32,48},{48,64},{64,80},{80,96},{96,112},{112,128},... | collective-permute-start | bytes 18440 | tf_op jit(solution)/shard_map/ppermute | solution.py:16
  230.7 0.8 copy-start.1
  258.2 71.6 %copy-start.2 = (bf16[512,512]{1,0:T(8,128)(2,1)S(1)}, bf16[512,512]{1,0:T(8,128)(2,1)}, u32[]{:S(2)}) copy-start(bf16[512,512]{1,0:T(8,128)(2,1)} %copy-done.1) | copy-start | bytes 1572868
  258.2 71.6 %copy-start.3 = (bf16[512,512]{0,1:T(8,128)(2,1)S(1)}, bf16[512,512]{0,1:T(8,128)(2,1)}, u32[]{:S(2)}) copy-start(bf16[512,512]{0,1:T(8,128)(2,1)} %copy.31) | copy-start | bytes 1572868
  311.0 72.3 %copy-start.9 = (f32[512]{0:T(512)S(1)}, f32[512]{0:T(512)}, u32[]{:S(2)}) copy-start(f32[512]{0:T(512)} %param.27) | copy-start | bytes 6148
Sparse Core Ops, SparseCore 0:
  10.9 76.6 all-gather.8
  90.1 115.9 all-gather.6
  234.2 76.7 all-gather.10
where the time goes:
time: 392 us; the launch traced here: 391 us
  waiting for transfers between devices  198 us (51%)
  blocking collectives  91.2 us (23%)
  matrix products  46.4 us (12%)
  other arithmetic  24.9 us (6%)
  local copies, waits for them, and re-layouts  15.4 us (4%)
  between operations  13.4 us (3%)
    all_gather x1, waiting for transfers between devices, body(): lax.all_gather(zx_rows, 'ctx', axis=0, tiled=True)  107 us
    psum x1, blocking collectives, body(): group_sums = lax.psum(placed, 'head')  48.1 us
    all_gather x1, waiting for transfers between devices, prefix(): gathered = jax.tree.map(lambda a: lax.all_gather(a, axis), part)  44 us
    all_gather x1, waiting for transfers between devices, body(): lax.all_gather(bc_rows, 'ctx', axis=0, tiled=True)  42.5 us
    dot_general x3, matrix products, body(): jnp.dot(tokens, piece, preferred_element_type=jnp.float32)  30.3 us
    all_gather x1, blocking collectives, body(): lax.all_gather(w_dt, 'ctx', axis=0, tiled=True)  21.8 us
    all_gather x1, blocking collectives, prefix(): gathered = jax.tree.map(lambda a: lax.all_gather(a, axis), part)  21.3 us
    add x15, other arithmetic, combine(): jnp.exp(later[0])[:, None, None] * earlier[1] + later[1]  18.1 us
  transfers between devices with their start and end apart: 4, of which 4 were waited for; matrix products, arithmetic and copies ran while one was open for 9% of the time, Pallas kernels for 0%

commit v1 on v0

--- a/solution.py
+++ b/solution.py
@@ -8,6 +8,19 @@
 N = 256
 G = 8
 K = 4
+
+
+def gather_around(array, axis, dim):
+    ways = lax.axis_size(axis)
+    up = [(d, (d + 1) % ways) for d in range(ways)]
+    down = [(d, (d - 1) % ways) for d in range(ways)]
+    earlier, later = ([array], [array])
+    for _ in range(ways // 2):
+        earlier.append(lax.ppermute(earlier[-1], axis, up))
+    for _ in range((ways - 1) // 2):
+        later.append(lax.ppermute(later[-1], axis, down))
+    line = jnp.concatenate([*earlier[::-1], *later[1:]], axis=dim)
+    return jnp.roll(line, (lax.axis_index(axis) - ways // 2) * array.shape[dim], axis=dim)
 
 
 def passed_along(x, axis, by):
@@ -72,7 +85,7 @@
     pieces = (
         lax.all_gather(zx_rows, "ctx", axis=0, tiled=True),
         lax.all_gather(bc_rows, "ctx", axis=0, tiled=True),
-        lax.all_gather(w_dt, "ctx", axis=0, tiled=True),
+        gather_around(w_dt, "ctx", 0),
     )
     zx_sum, bc_sum, step_sum = tuple(
         (jnp.dot(tokens, piece, preferred_element_type=jnp.float32) for piece in pieces)

time: 392 us -> 393 us (level)
  starting transfers between devices: 1.56 us -> 42.6 us
  waiting for transfers between devices: 198 us -> 176 us
  blocking collectives: 91.2 us -> 69.7 us
    ppermute x0 -> x15, starting transfers between devices: none -> 41.2 us  [the longest x8 41.1 us: gather_around(): earlier.append(lax.ppermute(earlier[-1], axis, up))]
    all_gather x1, waiting for transfers between devices: 42.5 us -> 6.07 us  [body(): lax.all_gather(bc_rows, 'ctx', axis=0, tiled=True)]
    all_gather x1 -> x0, blocking collectives: 21.8 us -> none  [body(): lax.all_gather(w_dt, 'ctx', axis=0, tiled=True)]
    ppermute x0 -> x15, waiting for transfers between devices: none -> 14.6 us  [the longest x7 8.6 us: gather_around(): later.append(lax.ppermute(later[-1], axis, down))]
  transfers between devices with their start and end apart: 4 -> 19, of which waited for: 4 -> 18; matrix products, arithmetic and copies ran while one was open for 9% -> 9% of each run, Pallas kernels for 0% -> 0%
where the time goes in v1:
time: 393 us; the launch traced here: 391 us
  waiting for transfers between devices  176 us (45%)
  blocking collectives  69.7 us (18%)
  matrix products  46.6 us (12%)
  starting transfers between devices  42.6 us (11%)
  other arithmetic  24.9 us (6%)
  local copies, waits for them, and re-layouts  17.7 us (5%)
  between operations  13.5 us (3%)
    all_gather x1, waiting for transfers between devices, body(): lax.all_gather(zx_rows, 'ctx', axis=0, tiled=True)  107 us
    psum x1, blocking collectives, body(): group_sums = lax.psum(placed, 'head')  48.1 us
    all_gather x1, waiting for transfers between devices, prefix(): gathered = jax.tree.map(lambda a: lax.all_gather(a, axis), part)  43.8 us
    ppermute x8, starting transfers between devices, gather_around(): earlier.append(lax.ppermute(earlier[-1], axis, up))  41.1 us
    dot_general x3, matrix products, body(): jnp.dot(tokens, piece, preferred_element_type=jnp.float32)  30.4 us
    all_gather x1, blocking collectives, prefix(): gathered = jax.tree.map(lambda a: lax.all_gather(a, axis), part)  21.5 us
    add x15, other arithmetic, combine(): jnp.exp(later[0])[:, None, None] * earlier[1] + later[1]  18.1 us
    dot_general x1, matrix products, body(): inner = jnp.einsum('hts,shp->thp', weights, x_heads, precision=highest)  8.68 us
  transfers between devices with their start and end apart: 19, of which 18 were waited for; matrix products, arithmetic and copies ran while one was open for 9% of the time, Pallas kernels for 0%

profile of v1, /device:TPU:30, one launch (start us, length us, event | category | flops | bytes accessed | tf_op | source)
XLA Modules:
  0.0 391.3 jit_solution(8547712449785128680)
XLA Ops:
  6.5 3.3 constant_dynamic-slice_fusion.8
  9.8 0.9 copy.38
  10.8 2.5 copy.40
  13.4 1.9 collective-permute-start.1
  15.4 2.0 collective-permute-done.1
  17.4 5.2 %collective-permute-start.2 = (bf16[512,8]{0,1:T(8,128)(2,1)S(1)}, bf16[512,8]{0,1:T(8,128)(2,1)S(1)}, u32[]{:S(2)}, u32[]{:S(2)}) collective-permute-start(bf16[512,8]{0,1:T(8,128)(2,1)S(1)} %collective-permute-done.1), channel_id=1, source_target_pairs={{0,16},{16,32},{32,48},{48,64},{64,80},{80,96},{96,112},{112,128},... | collective-permute-start | bytes 24584 | tf_op jit(solution)/shard_map/ppermute | solution.py:19
  22.5 1.4 collective-permute-done.2
  23.9 5.6 %collective-permute-start.3 = (bf16[512,8]{0,1:T(8,128)(2,1)S(1)}, bf16[512,8]{0,1:T(8,128)(2,1)S(1)}, u32[]{:S(2)}, u32[]{:S(2)}) collective-permute-start(bf16[512,8]{0,1:T(8,128)(2,1)S(1)} %collective-permute-done.2), channel_id=1, source_target_pairs={{0,16},{16,32},{32,48},{48,64},{64,80},{80,96},{96,112},{112,128},... | collective-permute-start | bytes 24584 | tf_op jit(solution)/shard_map/ppermute | solution.py:19
  29.8 1.1 collective-permute-done.3
  30.9 5.7 %collective-permute-start.4 = (bf16[512,8]{0,1:T(8,128)(2,1)S(1)}, bf16[512,8]{0,1:T(8,128)(2,1)S(1)}, u32[]{:S(2)}, u32[]{:S(2)}) collective-permute-start(bf16[512,8]{0,1:T(8,128)(2,1)S(1)} %collective-permute-done.3), channel_id=1, source_target_pairs={{0,16},{16,32},{32,48},{48,64},{64,80},{80,96},{96,112},{112,128},... | collective-permute-start | bytes 24584 | tf_op jit(solution)/shard_map/ppermute | solution.py:19
  36.6 0.9 fusion.69
  38.0 5.6 %collective-permute-start.5 = (bf16[512,8]{0,1:T(8,128)(2,1)S(1)}, bf16[512,8]{0,1:T(8,128)(2,1)S(1)}, u32[]{:S(2)}, u32[]{:S(2)}) collective-permute-start(bf16[512,8]{0,1:T(8,128)(2,1)S(1)} %collective-permute-done.4), channel_id=1, source_target_pairs={{0,16},{16,32},{32,48},{48,64},{64,80},{80,96},{96,112},{112,128},... | collective-permute-start | bytes 24584 | tf_op jit(solution)/shard_map/ppermute | solution.py:19
  43.6 0.8 slice_bitcast_fusion.2
  44.6 0.4 collective-permute-done.5
  44.9 5.6 %collective-permute-start.6 = (bf16[512,8]{0,1:T(8,128)(2,1)S(1)}, bf16[512,8]{0,1:T(8,128)(2,1)S(1)}, u32[]{:S(2)}, u32[]{:S(2)}) collective-permute-start(bf16[512,8]{0,1:T(8,128)(2,1)S(1)} %collective-permute-done.5), channel_id=1, source_target_pairs={{0,16},{16,32},{32,48},{48,64},{64,80},{80,96},{96,112},{112,128},... | collective-permute-start | bytes 24584 | tf_op jit(solution)/shard_map/ppermute | solution.py:19
  50.5 0.8 constant_dynamic-slice_fusion.4
  51.5 0.4 collective-permute-done.6
  51.9 5.7 %collective-permute-start.7 = (bf16[512,8]{0,1:T(8,128)(2,1)S(1)}, bf16[512,8]{0,1:T(8,128)(2,1)S(1)}, u32[]{:S(2)}, u32[]{:S(2)}) collective-permute-start(bf16[512,8]{0,1:T(8,128)(2,1)S(1)} %collective-permute-done.6), channel_id=1, source_target_pairs={{0,16},{16,32},{32,48},{48,64},{64,80},{80,96},{96,112},{112,128},... | collective-permute-start | bytes 24584 | tf_op jit(solution)/shard_map/ppermute | solution.py:19
  57.6 1.2 collective-permute-done.13
  59.1 5.8 %collective-permute-start.8 = (bf16[512,8]{0,1:T(8,128)(2,1)S(1)}, bf16[512,8]{0,1:T(8,128)(2,1)S(1)}, u32[]{:S(2)}, u32[]{:S(2)}) collective-permute-start(bf16[512,8]{0,1:T(8,128)(2,1)S(1)} %collective-permute-done.7), channel_id=1, source_target_pairs={{0,16},{16,32},{32,48},{48,64},{64,80},{80,96},{96,112},{112,128},... | collective-permute-start | bytes 24584 | tf_op jit(solution)/shard_map/ppermute | solution.py:19
  64.9 0.7 constant_dynamic-slice_fusion.7
  65.6 0.5 collective-permute-done.14
  66.4 0.7 constant_dynamic-update-slice_fusion.23
  67.1 6.2 %collective-permute-done.15 = bf16[512,8]{0,1:T(8,128)(2,1)S(1)} collective-permute-done((bf16[512,8]{0,1:T(8,128)(2,1)S(1)}, bf16[512,8]{0,1:T(8,128)(2,1)S(1)}, u32[]{:S(2)}, u32[]{:S(2)}) %collective-permute-start.15) | collective-permute-done | bytes 8224 | tf_op jit(solution)/shard_map/ppermute | solution.py:21
  73.4 0.7 constant_dynamic-update-slice_fusion.7
  74.2 5.8 %convolution_add_fusion = f32[8,512]{1,0:T(8,128)S(1)} fusion(bf16[512,8192]{1,0:T(8,128)(2,1)} %param.15, bf16[16384,8]{0,1:T(8,128)(2,1)S(1)} %constant_dynamic-update-slice_fusion, s32[]{:T(128)S(6)} %select_n.59, f32[8]{0:T(128)S(1)} %get-tuple-element.93), kind=kOutput, calls=%fused_computation.30 | convolution fusion | flops 67112960 | bytes 8536580 | tf_op jit(solution)/shard_map/dot_general | solution.py:91
  80.1 1.1 reduce-window.6
  81.7 6.1 %all-gather.9.cloned.1.call-done = bf16[8192,1,512]{2,0,1:T(8,128)(2,1)} async-done(((bf16[512,1,512]{2,0,1:T(8,128)(2,1)}), bf16[8192,1,512]{2,0,1:T(8,128)(2,1)}) %all-gather.9.cloned.1.call-update) | async-done | bytes 8388624 | tf_op jit(solution)/shard_map/all_gather | solution.py:87
  87.8 10.2 %fusion.27 = bf16[512,512]{1,0:T(8,128)(2,1)S(1)} fusion(bf16[512,8192]{1,0:T(8,128)(2,1)} %param.15, bf16[8192,1,512]{2,0,1:T(8,128)(2,1)} %all-gather.9.cloned.1.call-done, f32[512]{0:T(512)S(1)} %bitcast.139), kind=kOutput, calls=%fused_computation.29 | convolution fusion | flops 4295491584 | bytes 17303552 | tf_op jit(solution)/shard_map/dot_general | solution.py:91
  98.1 0.8 copy-done.5
  98.9 107.4 %all-gather.7.cloned.1.call-done = bf16[8192,1024]{1,0:T(8,128)(2,1)} async-done(((bf16[512,1024]{1,0:T(8,128)(2,1)}), bf16[8192,1024]{1,0:T(8,128)(2,1)}) %all-gather.7.cloned.1.call-update) | async-done | bytes 16777232 | tf_op jit(solution)/shard_map/all_gather | solution.py:86
  206.2 14.3 %fusion.71 = f32[512,1024]{1,0:T(8,128)S(1)} fusion(bf16[512,8192]{1,0:T(8,128)(2,1)} %param.15, bf16[8192,1024]{1,0:T(8,128)(2,1)} %all-gather.7.cloned.1.call-done), kind=kOutput, calls=%fused_computation.149 | convolution fusion | flops 8589934592 | bytes 27262976 | tf_op jit(solution)/shard_map/dot_general | solution.py:91
  220.9 1.3 collective-permute-start
  222.4 4.1 %collective-permute-done = bf16[3,1024]{1,0:T(4,128)(2,1)S(1)} collective-permute-done((bf16[3,1024]{1,0:T(4,128)(2,1)S(1)}, bf16[3,1024]{1,0:T(4,128)(2,1)S(1)}, u32[]{:S(2)}, u32[]{:S(2)}) %collective-permute-start) | collective-permute-done | bytes 6176 | tf_op jit(solution)/shard_map/ppermute | solution.py:29
  226.7 1.5 multiply_convert_fusion.1
  228.2 2.1 copy.31
  230.2 0.7 multiply_convert_fusion
  230.9 0.8 copy-done.2
  231.7 2.5 fusion.30
  234.3 21.5 %all-gather.2 = f32[16,1,8]{2,1,0:T(1,128)S(1)} all-gather(f32[1,1,8]{2,1,0:T(1,128)S(1)} %bitcast.138), channel_id=1, replica_groups=mesh['ctx'=16,'head'=16] {'ctx'}, dimensions={0}, use_global_device_ids=true | all-gather | bytes 544 | tf_op jit(solution)/shard_map/all_gather | solution.py:34
  255.9 1.4 copy.35
  257.3 1.3 fusion.53
  258.7 8.7 %fusion.16 = f32[512,8,64]{0,2,1:T(8,128)} fusion(bf16[512,8,64]{0,2,1:T(8,128)(2,1)} %bitcast.119, f32[8,512]{1,0:T(8,128)S(1)} %get-tuple-element.83, f32[512,512]{1,0:T(8,128)S(1)} %fusion.53, f32[8,512]{1,0:T(8,128)S(1)} %add_bitcast_fusion.1, pred[512,512]{1,0:T(8,128)(4,1)S(1)} %iota_compare_fusion), kind=kOutput, calls=%fused_computation.21 | convolution fusion | flops 1621098496 | bytes 2916352 | tf_op jit(solution)/shard_map/hts,shp->thp/dot_general | solution.py:116
  267.4 43.8 %all-gather.11.cloned.1.call-done = f32[128,64,256]{2,1,0:T(8,128)} async-done(((f32[8,64,256]{2,1,0:T(8,128)}), f32[128,64,256]{2,1,0:T(8,128)}) %all-gather.11.cloned.1.call-update) | async-done | bytes 8388624 | tf_op jit(solution)/shard_map/all_gather | solution.py:34
  311.2 18.9 %while.12 = (s32[]{:T(128)}, f32[8]{0:T(128)S(1)}, f32[8,64,256]{2,1,0:T(8,128)S(1)}, s32[]{:T(128)}, f32[16,8]{1,0:T(8,128)S(1)}, /*index=5*/f32[16,8,64,256]{3,2,1,0:T(8,128)}, s32[]{:T(128)}, s32[]{:T(128)}, s32[]{:T(128)}) while((s32[]{:T(128)}, f32[8]{0:T(128)S(1)}, f32[8,64,256]{2,1,0:T(8,128)S(1)}, s32[]{:T(128)}, ...), condition=%wide.region_3.4_spmd, body=%wide.region_2.3_spmd.sunk | while | flops 262157 | bytes 1573167 | solution.py:42
  311.3 1.2 bitcast_add_fusion.3
  312.5 1.2 bitcast_add_fusion.3
  313.8 1.2 bitcast_add_fusion.3
  315.0 1.2 bitcast_add_fusion.3
  316.3 1.2 bitcast_add_fusion.3
  317.5 1.2 bitcast_add_fusion.3
  318.8 1.2 bitcast_add_fusion.3
  320.1 1.2 bitcast_add_fusion.3
  321.3 1.2 bitcast_add_fusion.3
  322.6 1.2 bitcast_add_fusion.3
  323.8 1.2 bitcast_add_fusion.3
  325.1 1.2 bitcast_add_fusion.3
  326.3 1.2 bitcast_add_fusion.3
  327.6 1.2 bitcast_add_fusion.3
  328.9 1.2 bitcast_add_fusion.3
  330.1 3.7 multiply_reduce_fusion
  333.8 1.6 copy.34
  335.4 48.1 %psum.7 = f32[8,512]{1,0:T(8,128)S(1)} all-reduce(f32[8,512]{1,0:T(8,128)S(1)} %broadcast_multiply_fusion), channel_id=1, replica_groups=mesh['ctx'=16,'head'=16] {'head'}, use_global_device_ids=true, to_apply=%region_5.6 | all-reduce | flops 4096 | bytes 32768 | tf_op jit(solution)/shard_map/psum | solution.py:142
  383.6 1.2 fusion.45
  (108 shorter events, 3.9 us)
Async XLA Ops:
  6.5 51.1 %copy-start = (bf16[3,8,512]{2,1,0:T(8,128)(2,1)S(1)}, bf16[3,8,512]{2,1,0:T(8,128)(2,1)}, u32[]{:S(2)}) copy-start(bf16[3,8,512]{2,1,0:T(8,128)(2,1)} %param.24) | copy-start | bytes 73732
  6.5 81.3 %all-gather.9.cloned.1.call-start = ((), (), s32[]{:S(2)}) async-start(), calls=%async_computation.1 | async-start | bytes 8912896 | tf_op jit(solution)/shard_map/all_gather | solution.py:87
  10.8 195.5 %all-gather.7.cloned.1.call-start = ((), (), s32[]{:S(2)}) async-start(), calls=%async_computation | async-start | bytes 17825792 | tf_op jit(solution)/shard_map/all_gather | solution.py:86
  13.4 297.8 %all-gather.11.cloned.1.call-start = ((), (), s32[]{:S(2)}) async-start(), calls=%async_computation.2 | async-start | bytes 8912896 | tf_op jit(solution)/shard_map/all_gather | solution.py:34
  13.4 3.9 %collective-permute-start.1 = (bf16[512,8]{0,1:T(8,128)(2,1)}, bf16[512,8]{0,1:T(8,128)(2,1)S(1)}, u32[]{:S(2)}, u32[]{:S(2)}) collective-permute-start(bf16[512,8]{0,1:T(8,128)(2,1)} %param.20), channel_id=1, source_target_pairs={{0,16},{16,32},{32,48},{48,64},{64,80},{80,96},{96,112},{112,128},... | collective-permute-start | bytes 24584 | tf_op jit(solution)/shard_map/ppermute | solution.py:19
  17.4 6.5 %collective-permute-start.2 = (bf16[512,8]{0,1:T(8,128)(2,1)S(1)}, bf16[512,8]{0,1:T(8,128)(2,1)S(1)}, u32[]{:S(2)}, u32[]{:S(2)}) collective-permute-start(bf16[512,8]{0,1:T(8,128)(2,1)S(1)} %collective-permute-done.1), channel_id=1, source_target_pairs={{0,16},{16,32},{32,48},{48,64},{64,80},{80,96},{96,112},{112,128},... | collective-permute-start | bytes 24584 | tf_op jit(solution)/shard_map/ppermute | solution.py:19
  22.5 7.3 %collective-permute-start.9 = (bf16[512,8]{0,1:T(8,128)(2,1)}, bf16[512,8]{0,1:T(8,128)(2,1)S(1)}, u32[]{:S(2)}, u32[]{:S(2)}) collective-permute-start(bf16[512,8]{0,1:T(8,128)(2,1)} %param.20), channel_id=1, source_target_pairs={{0,240},{16,0},{32,16},{48,32},{64,48},{80,64},{96,80},{112,96},{1... | collective-permute-start | bytes 24584 | tf_op jit(solution)/shard_map/ppermute | solution.py:21
  23.9 7.0 %collective-permute-start.3 = (bf16[512,8]{0,1:T(8,128)(2,1)S(1)}, bf16[512,8]{0,1:T(8,128)(2,1)S(1)}, u32[]{:S(2)}, u32[]{:S(2)}) collective-permute-start(bf16[512,8]{0,1:T(8,128)(2,1)S(1)} %collective-permute-done.2), channel_id=1, source_target_pairs={{0,16},{16,32},{32,48},{48,64},{64,80},{80,96},{96,112},{112,128},... | collective-permute-start | bytes 24584 | tf_op jit(solution)/shard_map/ppermute | solution.py:19
  29.8 7.7 %collective-permute-start.10 = (bf16[512,8]{0,1:T(8,128)(2,1)S(1)}, bf16[512,8]{0,1:T(8,128)(2,1)S(1)}, u32[]{:S(2)}, u32[]{:S(2)}) collective-permute-start(bf16[512,8]{0,1:T(8,128)(2,1)S(1)} %collective-permute-done.9), channel_id=1, source_target_pairs={{0,240},{16,0},{32,16},{48,32},{64,48},{80,64},{96,80},{112,96},{1... | collective-permute-start | bytes 24584 | tf_op jit(solution)/shard_map/ppermute | solution.py:21
  30.9 7.1 %collective-permute-start.4 = (bf16[512,8]{0,1:T(8,128)(2,1)S(1)}, bf16[512,8]{0,1:T(8,128)(2,1)S(1)}, u32[]{:S(2)}, u32[]{:S(2)}) collective-permute-start(bf16[512,8]{0,1:T(8,128)(2,1)S(1)} %collective-permute-done.3), channel_id=1, source_target_pairs={{0,16},{16,32},{32,48},{48,64},{64,80},{80,96},{96,112},{112,128},... | collective-permute-start | bytes 24584 | tf_op jit(solution)/shard_map/ppermute | solution.py:19
  37.5 7.0 %collective-permute-start.11 = (bf16[512,8]{0,1:T(8,128)(2,1)S(1)}, bf16[512,8]{0,1:T(8,128)(2,1)S(1)}, u32[]{:S(2)}, u32[]{:S(2)}) collective-permute-start(bf16[512,8]{0,1:T(8,128)(2,1)S(1)} %collective-permute-done.10), channel_id=1, source_target_pairs={{0,240},{16,0},{32,16},{48,32},{64,48},{80,64},{96,80},{112,96},{1... | collective-permute-start | bytes 24584 | tf_op jit(solution)/shard_map/ppermute | solution.py:21
  38.0 7.0 %collective-permute-start.5 = (bf16[512,8]{0,1:T(8,128)(2,1)S(1)}, bf16[512,8]{0,1:T(8,128)(2,1)S(1)}, u32[]{:S(2)}, u32[]{:S(2)}) collective-permute-start(bf16[512,8]{0,1:T(8,128)(2,1)S(1)} %collective-permute-done.4), channel_id=1, source_target_pairs={{0,16},{16,32},{32,48},{48,64},{64,80},{80,96},{96,112},{112,128},... | collective-permute-start | bytes 24584 | tf_op jit(solution)/shard_map/ppermute | solution.py:19
  44.6 7.0 %collective-permute-start.12 = (bf16[512,8]{0,1:T(8,128)(2,1)S(1)}, bf16[512,8]{0,1:T(8,128)(2,1)S(1)}, u32[]{:S(2)}, u32[]{:S(2)}) collective-permute-start(bf16[512,8]{0,1:T(8,128)(2,1)S(1)} %collective-permute-done.11), channel_id=1, source_target_pairs={{0,240},{16,0},{32,16},{48,32},{64,48},{80,64},{96,80},{112,96},{1... | collective-permute-start | bytes 24584 | tf_op jit(solution)/shard_map/ppermute | solution.py:21
  44.9 7.0 %collective-permute-start.6 = (bf16[512,8]{0,1:T(8,128)(2,1)S(1)}, bf16[512,8]{0,1:T(8,128)(2,1)S(1)}, u32[]{:S(2)}, u32[]{:S(2)}) collective-permute-start(bf16[512,8]{0,1:T(8,128)(2,1)S(1)} %collective-permute-done.5), channel_id=1, source_target_pairs={{0,16},{16,32},{32,48},{48,64},{64,80},{80,96},{96,112},{112,128},... | collective-permute-start | bytes 24584 | tf_op jit(solution)/shard_map/ppermute | solution.py:19
  51.5 7.3 %collective-permute-start.13 = (bf16[512,8]{0,1:T(8,128)(2,1)S(1)}, bf16[512,8]{0,1:T(8,128)(2,1)S(1)}, u32[]{:S(2)}, u32[]{:S(2)}) collective-permute-start(bf16[512,8]{0,1:T(8,128)(2,1)S(1)} %collective-permute-done.12), channel_id=1, source_target_pairs={{0,240},{16,0},{32,16},{48,32},{64,48},{80,64},{96,80},{112,96},{1... | collective-permute-start | bytes 24584 | tf_op jit(solution)/shard_map/ppermute | solution.py:21
  51.9 7.2 %collective-permute-start.7 = (bf16[512,8]{0,1:T(8,128)(2,1)S(1)}, bf16[512,8]{0,1:T(8,128)(2,1)S(1)}, u32[]{:S(2)}, u32[]{:S(2)}) collective-permute-start(bf16[512,8]{0,1:T(8,128)(2,1)S(1)} %collective-permute-done.6), channel_id=1, source_target_pairs={{0,16},{16,32},{32,48},{48,64},{64,80},{80,96},{96,112},{112,128},... | collective-permute-start | bytes 24584 | tf_op jit(solution)/shard_map/ppermute | solution.py:19
  58.8 7.3 %collective-permute-start.14 = (bf16[512,8]{0,1:T(8,128)(2,1)S(1)}, bf16[512,8]{0,1:T(8,128)(2,1)S(1)}, u32[]{:S(2)}, u32[]{:S(2)}) collective-permute-start(bf16[512,8]{0,1:T(8,128)(2,1)S(1)} %collective-permute-done.13), channel_id=1, source_target_pairs={{0,240},{16,0},{32,16},{48,32},{64,48},{80,64},{96,80},{112,96},{1... | collective-permute-start | bytes 24584 | tf_op jit(solution)/shard_map/ppermute | solution.py:21
  59.1 7.3 %collective-permute-start.8 = (bf16[512,8]{0,1:T(8,128)(2,1)S(1)}, bf16[512,8]{0,1:T(8,128)(2,1)S(1)}, u32[]{:S(2)}, u32[]{:S(2)}) collective-permute-start(bf16[512,8]{0,1:T(8,128)(2,1)S(1)} %collective-permute-done.7), channel_id=1, source_target_pairs={{0,16},{16,32},{32,48},{48,64},{64,80},{80,96},{96,112},{112,128},... | collective-permute-start | bytes 24584 | tf_op jit(solution)/shard_map/ppermute | solution.py:19
  66.1 7.3 %collective-permute-start.15 = (bf16[512,8]{0,1:T(8,128)(2,1)S(1)}, bf16[512,8]{0,1:T(8,128)(2,1)S(1)}, u32[]{:S(2)}, u32[]{:S(2)}) collective-permute-start(bf16[512,8]{0,1:T(8,128)(2,1)S(1)} %collective-permute-done.14), channel_id=1, source_target_pairs={{0,240},{16,0},{32,16},{48,32},{64,48},{80,64},{96,80},{112,96},{1... | collective-permute-start | bytes 24584 | tf_op jit(solution)/shard_map/ppermute | solution.py:21
  98.1 0.8 copy-start.5
  98.9 121.7 %copy-start.7 = (f32[2,512]{1,0:T(2,128)S(1)}, f32[2,512]{1,0:T(2,128)}, u32[]{:S(2)}) copy-start(f32[2,512]{1,0:T(2,128)} %param.17) | copy-start | bytes 12292
  98.9 127.6 %copy-start.8 = (bf16[3,512]{1,0:T(4,128)(2,1)S(1)}, bf16[3,512]{1,0:T(4,128)(2,1)}, u32[]{:S(2)}) copy-start(bf16[3,512]{1,0:T(4,128)(2,1)} %param.23) | copy-start | bytes 9220
  206.2 20.2 %copy-start.6 = (bf16[512,512]{1,0:T(8,128)(2,1)S(1)}, bf16[512,512]{1,0:T(8,128)(2,1)}, u32[]{:S(2)}) copy-start(bf16[512,512]{1,0:T(8,128)(2,1)} %copy-done.5) | copy-start | bytes 1572868
  220.9 5.5 %collective-permute-start = (bf16[3,1024]{1,0:T(4,128)(2,1)S(1)}, bf16[3,1024]{1,0:T(4,128)(2,1)S(1)}, u32[]{:S(2)}, u32[]{:S(2)}) collective-permute-start(bf16[3,1024]{1,0:T(4,128)(2,1)S(1)} %pad_maximum_fusion), channel_id=1, source_target_pairs={{0,16},{16,32},{32,48},{48,64},{64,80},{80,96},{96,112},{112,128},... | collective-permute-start | bytes 18440 | tf_op jit(solution)/shard_map/ppermute | solution.py:29
  230.9 0.8 copy-start.2
  258.7 71.4 %copy-start.3 = (bf16[512,512]{1,0:T(8,128)(2,1)S(1)}, bf16[512,512]{1,0:T(8,128)(2,1)}, u32[]{:S(2)}) copy-start(bf16[512,512]{1,0:T(8,128)(2,1)} %copy-done.2) | copy-start | bytes 1572868
  258.7 71.4 %copy-start.4 = (bf16[512,512]{0,1:T(8,128)(2,1)S(1)}, bf16[512,512]{0,1:T(8,128)(2,1)}, u32[]{:S(2)}) copy-start(bf16[512,512]{0,1:T(8,128)(2,1)} %copy.31) | copy-start | bytes 1572868
  311.2 73.6 %copy-start.1 = (bf16[3,8,512]{2,1,0:T(8,128)(2,1)S(1)}, bf16[3,8,512]{2,1,0:T(8,128)(2,1)}, u32[]{:S(2)}) copy-start(bf16[3,8,512]{2,1,0:T(8,128)(2,1)} %param.24) | copy-start | bytes 73732
  311.2 72.4 %copy-start.9 = (f32[512]{0:T(512)S(1)}, f32[512]{0:T(512)}, u32[]{:S(2)}) copy-start(f32[512]{0:T(512)} %param.27) | copy-start | bytes 6148
Sparse Core Ops, SparseCore 0:
  10.9 76.8 all-gather.8
  90.2 115.9 all-gather.6
  234.3 76.7 all-gather.10
